TPU v7x, 32 devices: a whole 2x2x4 slice. The times are simulated.
32 devices in a mesh: gx: 16 (over z, y, core), gy: 2 (over x).
Axes of the slice: x: 2, y: 2, z: 4, core: 2. Of those that a mesh axis runs over, the one named last changes fastest.
Arguments:
- velocity: float32 [3, 256, 32, 128], P(None, 'gx', 'gy'), may hold values from -6 to 6
- pressure: float32 [256, 32, 128], P('gx', 'gy'), may hold values from -6 to 6
- land_type: int32 [256, 32], P('gx', 'gy'), may hold values from 0 to 15
- turbine_cells: int32 [256, 32, 128], P('gx', 'gy'), may hold values 0 or 1
- surface_drag: float32 [16], replicated, may hold values from 0.2 to 2
Outputs:
- velocity_new: float32 [3, 256, 32, 128], P(None, 'gx', 'gy')
- pressure_new: float32 [256, 32, 128], P('gx', 'gy')
All inputs are finite; a program needn't handle non-finite values. No bound on the sum of `turbine_cells` on one device may be relied on, other than what follows from the above.
Results may differ from a plain program's by a relative error of at most 0.00002.
Values sent between devices are 32-bit elements; how exact they have to be, the bound alone decides.
A program may use at most 64 MiB of HBM per device.

v0:
```python
import jax
import jax.numpy as jnp
from jax import lax
from jax.sharding import PartitionSpec as P

SWEEPS = 2
COARSE_SWEEPS = 4


time_step = 0.1
vertical_step = 0.5
eddy_coeff = 0.03
thrust_factor = 2.0
relax_weight = 0.8
driving_force = 1.0


def with_halo(block, sides, width):
    for axis, dim in sides:
        count = lax.axis_size(axis)
        forward = [(i, i + 1) for i in range(count - 1)]
        forward.append((count - 1, 0))
        backward = [(target, source) for source, target in forward]
        low = lax.ppermute(
            lax.slice_in_dim(block, block.shape[dim] - width, None, axis=dim), axis, forward
        )
        high = lax.ppermute(lax.slice_in_dim(block, 0, width, axis=dim), axis, backward)
        block = jnp.concatenate([low, block, high], axis=dim)
    return block


def shifted(values, axis_pos, offset):
    starts = [1, 1, 1]
    starts[axis_pos] = 1 + offset
    length = [values.shape[-3] - 2, values.shape[-2] - 2, values.shape[-1] - 2]
    return values[
        ...,
        starts[0] : starts[0] + length[0],
        starts[1] : starts[1] + length[1],
        starts[2] : starts[2] + length[2],
    ]


def central(values, axis_pos):
    spacing = vertical_step if axis_pos == 2 else 1.0
    return (shifted(values, axis_pos, 1) - shifted(values, axis_pos, -1)) * (0.5 / spacing)


def surface_field(land_type, turbine_cells, surface_drag):
    kind_ids = jnp.arange(surface_drag.shape[0], dtype=jnp.int32)
    ground = jnp.sum(jnp.where(land_type[:, :, None] == kind_ids, surface_drag, 0.0), axis=-1)
    ground_layer = jnp.arange(turbine_cells.shape[2], dtype=jnp.int32) == 0
    return thrust_factor * turbine_cells.astype(jnp.float32) + jnp.where(
        ground_layer, ground[:, :, None], 0.0
    )


def advance(padded, drag_field):
    gradient = [central(padded, axis_pos) for axis_pos in range(3)]
    strain = [
        [0.5 * (gradient[col_idx][row_idx] + gradient[row_idx][col_idx]) for col_idx in range(3)]
        for row_idx in range(3)
    ]
    square_sum = strain[0][0] * strain[0][0]
    for row_idx in range(3):
        for col_idx in range(3):
            if row_idx + col_idx > 0:
                square_sum = square_sum + strain[row_idx][col_idx] * strain[row_idx][col_idx]
    viscosity = eddy_coeff * jnp.sqrt(2.0 * square_sum)
    centre = padded[:, 2:-2, 2:-2, 2:-2]
    wind_speed = jnp.sqrt(centre[0] * centre[0] + centre[1] * centre[1])
    updated = []
    for row_idx in range(3):
        change = jnp.zeros_like(centre[0])
        for col_idx in range(3):
            stress = 2.0 * viscosity * strain[row_idx][col_idx]
            change = (
                change
                + central(stress, col_idx)
                - centre[col_idx] * gradient[col_idx][row_idx][1:-1, 1:-1, 1:-1]
            )
        if row_idx < 2:
            change = change - drag_field * wind_speed * centre[row_idx]
        if row_idx == 0:
            change = change + driving_force
        updated.append(centre[row_idx] + time_step * change)
    return jnp.stack(updated)


def divergence(padded):
    return central(padded[0], 0) + central(padded[1], 1) + central(padded[2], 2)


def laplace(padded, spacing):
    centre = padded[1:-1, 1:-1, 1:-1]
    upright = vertical_step * spacing
    horizontal = (
        shifted(padded, 0, 1)
        + shifted(padded, 0, -1)
        + shifted(padded, 1, 1)
        + shifted(padded, 1, -1)
        - 4.0 * centre
    ) / (spacing * spacing)
    vertical = (shifted(padded, 2, 1) + shifted(padded, 2, -1) - 2.0 * centre) / (upright * upright)
    return horizontal + vertical


def diagonal_of(spacing):
    upright = vertical_step * spacing
    return -(4.0 / (spacing * spacing) + 2.0 / (upright * upright))


def relax(pressure, padded, source, spacing):
    return pressure + relax_weight * (source - laplace(padded, spacing)) / diagonal_of(spacing)


def line_correct(pressure, residual, spacing):
    return pressure + relax_weight * jnp.mean(residual, axis=1, keepdims=True) / diagonal_of(
        spacing
    )


def coarsen(values):
    return values.reshape(
        values.shape[0] // 2, 2, values.shape[1] // 2, 2, values.shape[2] // 2, 2
    ).mean(axis=(1, 3, 5))


def refine(values):
    return jnp.repeat(jnp.repeat(jnp.repeat(values, 2, axis=0), 2, axis=1), 2, axis=2)


def faces(values):
    padded = with_halo(values, (("gx", 0), ("gy", 1)), 1)
    return jnp.pad(padded, ((0, 0), (0, 0), (1, 1)), mode="edge")


def strip(values):
    padded = with_halo(values, (("gx", 0),), 1)
    padded = jnp.pad(padded, ((0, 0), (1, 1), (0, 0)), mode="wrap")
    return jnp.pad(padded, ((0, 0), (0, 0), (1, 1)), mode="edge")


def smooth(pressure, source, spacing, padder, count):
    for sweep_idx in range(count):
        pressure = relax(pressure, padder(pressure), source, spacing)
    return pressure


def residual_of(pressure, source, spacing, padder):
    return source - laplace(padder(pressure), spacing)


def per_device(velocity, pressure, land_type, turbine_cells, surface_drag):
    drag_field = surface_field(land_type, turbine_cells, surface_drag)
    stacked = jnp.concatenate([velocity, drag_field[None]], 0)
    widened = with_halo(stacked, (("gx", 1), ("gy", 2)), 3)
    moving = jnp.pad(widened[:3], ((0, 0), (0, 0), (0, 0), (2, 2)))
    star_rim = advance(moving, widened[3, 2:-2, 2:-2])
    star_velocity = star_rim[:, 1:-1, 1:-1]
    source = divergence(jnp.pad(star_rim, ((0, 0), (0, 0), (0, 0), (1, 1)))) / time_step
    finest = smooth(pressure, source, 1.0, faces, SWEEPS)
    source_one = coarsen(residual_of(finest, source, 1.0, faces))
    second = smooth(jnp.zeros_like(source_one), source_one, 2.0, faces, SWEEPS)
    local_two = coarsen(residual_of(second, source_one, 2.0, faces))
    source_two = lax.all_gather(local_two, "gy", axis=1, tiled=True)
    third = smooth(jnp.zeros_like(source_two), source_two, 4.0, strip, SWEEPS)
    source_three = coarsen(residual_of(third, source_two, 4.0, strip))
    coarsest = smooth(jnp.zeros_like(source_three), source_three, 8.0, strip, COARSE_SWEEPS)
    coarsest = line_correct(coarsest, residual_of(coarsest, source_three, 8.0, strip), 8.0)
    third = smooth(third + refine(coarsest), source_two, 4.0, strip, SWEEPS)
    own_third = lax.dynamic_slice_in_dim(
        third, lax.axis_index("gy") * local_two.shape[1], local_two.shape[1], 1
    )
    second = smooth(second + refine(own_third), source_one, 2.0, faces, SWEEPS)
    pressure_new = smooth(finest + refine(second), source, 1.0, faces, SWEEPS)
    padded = faces(pressure_new)
    gradient = jnp.stack([central(padded, 0), central(padded, 1), central(padded, 2)])
    return (star_velocity - time_step * gradient, pressure_new)


def solution(mesh):
    in_specs = (
        P(None, "gx", "gy", None),
        P("gx", "gy", None),
        P("gx", "gy"),
        P("gx", "gy", None),
        P(),
    )
    out_specs = (P(None, "gx", "gy", None), P("gx", "gy", None))
    return jax.shard_map(
        per_device, mesh=mesh, in_specs=in_specs, out_specs=out_specs, check_vma=False
    )
```

profile of v0, /device:TPU:0, one launch (start us, length us, event | category | flops | bytes accessed | tf_op | source)
XLA Modules:
  0.0 220.4 jit_solution(6077925993191126964)
XLA Ops:
  0.7 5.5 %collective-permute-start.16 = (f32[1,8,64]{2,1,0:T(8,128)S(1)}, f32[1,8,64]{2,1,0:T(8,128)S(1)}, u32[]{:S(2)}, u32[]{:S(2)}) collective-permute-start(f32[1,8,64]{2,1,0:T(8,128)S(1)} %broadcast.203), channel_id=1, source_target_pairs={{2,0},{4,2},{6,4},{8,6},{10,8},{12,10},{14,12},{16,14},{18,16},{20... | collective-permute-start | bytes 6152 | tf_op jit(solution)/shard_map/ppermute | solution.py:27
  6.2 4.4 %collective-permute-start.34 = (f32[1,4,16]{2,1,0:T(4,128)S(1)}, f32[1,4,16]{2,1,0:T(4,128)S(1)}, u32[]{:S(2)}, u32[]{:S(2)}) collective-permute-start(f32[1,4,16]{2,1,0:T(4,128)S(1)} %broadcast.212), channel_id=1, source_target_pairs={{2,0},{4,2},{6,4},{8,6},{10,8},{12,10},{14,12},{16,14},{18,16},{20... | collective-permute-start | bytes 776 | tf_op jit(solution)/shard_map/ppermute | solution.py:27
  14.2 2.9 %collective-permute-done.5 = f32[1,16,128]{2,1,0:T(8,128)S(1)} collective-permute-done((f32[1,16,128]{2,1,0:T(8,128)S(1)}, f32[1,16,128]{2,1,0:T(8,128)S(1)}, u32[]{:S(2)}, u32[]{:S(2)}) %collective-permute-start.5) | collective-permute-done | bytes 8224 | tf_op jit(solution)/shard_map/ppermute | solution.py:24
  17.1 1.6 collective-permute-start.4
  20.1 1.6 collective-permute-start.6
  22.2 1.6 collective-permute-done.6
  23.8 3.4 %collective-permute-start.1 = (f32[4,3,16,128]{3,2,1,0:T(8,128)S(1)}, f32[4,3,16,128]{3,2,1,0:T(8,128)S(1)}, u32[]{:S(2)}, u32[]{:S(2)}) collective-permute-start(f32[4,3,16,128]{3,2,1,0:T(8,128)S(1)} %get-tuple-element.45), channel_id=1, source_target_pairs={{2,0},{4,2},{6,4},{8,6},{10,8},{12,10},{14,12},{16,14},{18,16},{20... | collective-permute-start | bytes 294920 | tf_op jit(solution)/shard_map/ppermute | solution.py:27
  27.2 1.7 collective-permute-start.28
  29.5 1.6 collective-permute-start.2
  31.9 3.1 %collective-permute-done.2 = f32[4,22,3,128]{3,0,2,1:T(4,128)S(1)} collective-permute-done((f32[4,22,3,128]{3,0,2,1:T(4,128)S(1)}, f32[4,22,3,128]{3,0,2,1:T(4,128)S(1)}, u32[]{:S(2)}, u32[]{:S(2)}) %collective-permute-start.2) | collective-permute-done | bytes 135200 | tf_op jit(solution)/shard_map/ppermute | solution.py:24
  35.0 1.4 collective-permute-done.3
  36.7 2.0 fusion.3
  43.0 3.8 %collective-permute-start.8 = (f32[1,16,128]{2,1,0:T(8,128)S(1)}, f32[1,16,128]{2,1,0:T(8,128)S(1)}, u32[]{:S(2)}, u32[]{:S(2)}) collective-permute-start(f32[1,16,128]{2,1,0:T(8,128)S(1)} %get-tuple-element.81), channel_id=1, source_target_pairs={{2,0},{4,2},{6,4},{8,6},{10,8},{12,10},{14,12},{16,14},{18,16},{20... | collective-permute-start | bytes 24584 | tf_op jit(solution)/shard_map/ppermute | solution.py:27
  48.2 4.4 %collective-permute-done.9 = f32[1,16,128]{2,1,0:T(8,128)S(1)} collective-permute-done((f32[1,16,128]{2,1,0:T(8,128)S(1)}, f32[1,16,128]{2,1,0:T(8,128)S(1)}, u32[]{:S(2)}, u32[]{:S(2)}) %collective-permute-start.9) | collective-permute-done | bytes 8224 | tf_op jit(solution)/shard_map/ppermute | solution.py:24
  52.6 1.4 collective-permute-start.10
  54.7 1.4 collective-permute-start.18
  59.8 4.2 %collective-permute-done.13 = f32[1,16,128]{2,1,0:T(8,128)S(1)} collective-permute-done((f32[1,16,128]{2,1,0:T(8,128)S(1)}, f32[1,16,128]{2,1,0:T(8,128)S(1)}, u32[]{:S(2)}, u32[]{:S(2)}) %collective-permute-start.13) | collective-permute-done | bytes 8224 | tf_op jit(solution)/shard_map/ppermute | solution.py:24
  64.7 1.3 collective-permute-start.15
  66.2 1.6 collective-permute-done.14
  68.8 9.8 %reshape.47 = f32[8,2,8,2,64,2]{5,4,3,2,1,0:T(8,128)} reshape(f32[16,16,128]{2,1,0:T(8,128)S(1)} %fusion.82) | data formatting | bytes 262144 | tf_op jit(solution)/shard_map/reshape | solution.py:124
  78.6 4.0 %reduce_sum.46 = f32[8,8,64]{2,1,0:T(8,128)S(1)} reduce(f32[8,2,8,2,64,2]{5,4,3,2,1,0:T(8,128)} %reshape.47, f32[]{:T(128)} %constant.138.clone.1), dimensions={1,3,5}, to_apply=%region_1.2 | reduce | flops 28672 | bytes 147460 | tf_op jit(solution)/shard_map/reduce_sum | solution.py:126
  84.1 4.6 %collective-permute-done.21 = f32[1,8,64]{2,1,0:T(8,128)S(1)} collective-permute-done((f32[1,8,64]{2,1,0:T(8,128)S(1)}, f32[1,8,64]{2,1,0:T(8,128)S(1)}, u32[]{:S(2)}, u32[]{:S(2)}) %collective-permute-start.21) | collective-permute-done | bytes 2080 | tf_op jit(solution)/shard_map/ppermute | solution.py:24
  88.8 1.4 collective-permute-start.22
  90.9 1.6 collective-permute-done.22
  95.4 4.5 %collective-permute-done.25 = f32[1,8,64]{2,1,0:T(8,128)S(1)} collective-permute-done((f32[1,8,64]{2,1,0:T(8,128)S(1)}, f32[1,8,64]{2,1,0:T(8,128)S(1)}, u32[]{:S(2)}, u32[]{:S(2)}) %collective-permute-start.25) | collective-permute-done | bytes 2080 | tf_op jit(solution)/shard_map/ppermute | solution.py:24
  100.6 1.3 collective-permute-start.27
  105.8 4.4 %all_gather.3 = f32[4,8,32]{2,0,1:T(4,128)S(1)} all-gather(f32[4,4,32]{2,0,1:T(4,128)S(1)} %copy.529), channel_id=1, replica_groups=mesh['gx'=16,'gy'=2] {'gy'}, dimensions={1}, use_global_device_ids=true | all-gather | bytes 6144 | tf_op jit(solution)/shard_map/all_gather | solution.py:166
  111.9 4.5 %collective-permute-done.31 = f32[1,8,32]{1,2,0:T(8,128)S(1)} collective-permute-done((f32[1,8,32]{1,2,0:T(8,128)S(1)}, f32[1,8,32]{1,2,0:T(8,128)S(1)}, u32[]{:S(2)}, u32[]{:S(2)}) %collective-permute-start.31) | collective-permute-done | bytes 1056 | tf_op jit(solution)/shard_map/ppermute | solution.py:24
  118.8 4.5 %collective-permute-done.33 = f32[1,8,32]{1,2,0:T(8,128)S(1)} collective-permute-done((f32[1,8,32]{1,2,0:T(8,128)S(1)}, f32[1,8,32]{1,2,0:T(8,128)S(1)}, u32[]{:S(2)}, u32[]{:S(2)}) %collective-permute-start.33) | collective-permute-done | bytes 1056 | tf_op jit(solution)/shard_map/ppermute | solution.py:24
  126.1 4.5 %collective-permute-done.37 = f32[1,4,16]{2,1,0:T(4,128)S(1)} collective-permute-done((f32[1,4,16]{2,1,0:T(4,128)S(1)}, f32[1,4,16]{2,1,0:T(4,128)S(1)}, u32[]{:S(2)}, u32[]{:S(2)}) %collective-permute-start.37) | collective-permute-done | bytes 288 | tf_op jit(solution)/shard_map/ppermute | solution.py:24
  132.1 4.5 %collective-permute-done.39 = f32[1,4,16]{2,1,0:T(4,128)S(1)} collective-permute-done((f32[1,4,16]{2,1,0:T(4,128)S(1)}, f32[1,4,16]{2,1,0:T(4,128)S(1)}, u32[]{:S(2)}, u32[]{:S(2)}) %collective-permute-start.39) | collective-permute-done | bytes 288 | tf_op jit(solution)/shard_map/ppermute | solution.py:24
  138.2 4.5 %collective-permute-done.41 = f32[1,4,16]{2,1,0:T(4,128)S(1)} collective-permute-done((f32[1,4,16]{2,1,0:T(4,128)S(1)}, f32[1,4,16]{2,1,0:T(4,128)S(1)}, u32[]{:S(2)}, u32[]{:S(2)}) %collective-permute-start.41) | collective-permute-done | bytes 288 | tf_op jit(solution)/shard_map/ppermute | solution.py:24
  144.2 4.5 %collective-permute-done.43 = f32[1,4,16]{2,1,0:T(4,128)S(1)} collective-permute-done((f32[1,4,16]{2,1,0:T(4,128)S(1)}, f32[1,4,16]{2,1,0:T(4,128)S(1)}, u32[]{:S(2)}, u32[]{:S(2)}) %collective-permute-start.43) | collective-permute-done | bytes 288 | tf_op jit(solution)/shard_map/ppermute | solution.py:24
  150.6 4.5 %collective-permute-done.45 = f32[1,8,32]{1,2,0:T(8,128)S(1)} collective-permute-done((f32[1,8,32]{1,2,0:T(8,128)S(1)}, f32[1,8,32]{1,2,0:T(8,128)S(1)}, u32[]{:S(2)}, u32[]{:S(2)}) %collective-permute-start.45) | collective-permute-done | bytes 1056 | tf_op jit(solution)/shard_map/ppermute | solution.py:24
  157.5 4.5 %collective-permute-done.47 = f32[1,8,32]{1,2,0:T(8,128)S(1)} collective-permute-done((f32[1,8,32]{1,2,0:T(8,128)S(1)}, f32[1,8,32]{1,2,0:T(8,128)S(1)}, u32[]{:S(2)}, u32[]{:S(2)}) %collective-permute-start.47) | collective-permute-done | bytes 1056 | tf_op jit(solution)/shard_map/ppermute | solution.py:24
  164.9 4.5 %collective-permute-done.49 = f32[1,8,64]{2,1,0:T(8,128)S(1)} collective-permute-done((f32[1,8,64]{2,1,0:T(8,128)S(1)}, f32[1,8,64]{2,1,0:T(8,128)S(1)}, u32[]{:S(2)}, u32[]{:S(2)}) %collective-permute-start.49) | collective-permute-done | bytes 2080 | tf_op jit(solution)/shard_map/ppermute | solution.py:24
  169.4 1.4 collective-permute-start.50
  171.5 1.6 collective-permute-done.50
  176.1 4.5 %collective-permute-done.53 = f32[1,8,64]{2,1,0:T(8,128)S(1)} collective-permute-done((f32[1,8,64]{2,1,0:T(8,128)S(1)}, f32[1,8,64]{2,1,0:T(8,128)S(1)}, u32[]{:S(2)}, u32[]{:S(2)}) %collective-permute-start.53) | collective-permute-done | bytes 2080 | tf_op jit(solution)/shard_map/ppermute | solution.py:24
  182.6 1.6 collective-permute-done.54
  187.5 4.5 %collective-permute-done.57 = f32[1,16,128]{2,1,0:T(8,128)S(1)} collective-permute-done((f32[1,16,128]{2,1,0:T(8,128)S(1)}, f32[1,16,128]{2,1,0:T(8,128)S(1)}, u32[]{:S(2)}, u32[]{:S(2)}) %collective-permute-start.57) | collective-permute-done | bytes 8224 | tf_op jit(solution)/shard_map/ppermute | solution.py:24
  192.0 1.4 collective-permute-start.58
  194.1 1.6 collective-permute-done.58
  198.9 4.5 %collective-permute-done.61 = f32[1,16,128]{2,1,0:T(8,128)S(1)} collective-permute-done((f32[1,16,128]{2,1,0:T(8,128)S(1)}, f32[1,16,128]{2,1,0:T(8,128)S(1)}, u32[]{:S(2)}, u32[]{:S(2)}) %collective-permute-start.61) | collective-permute-done | bytes 8224 | tf_op jit(solution)/shard_map/ppermute | solution.py:24
  205.5 1.6 collective-permute-done.62
  209.6 4.5 %collective-permute-done.65 = f32[1,16,128]{2,1,0:T(8,128)S(1)} collective-permute-done((f32[1,16,128]{2,1,0:T(8,128)S(1)}, f32[1,16,128]{2,1,0:T(8,128)S(1)}, u32[]{:S(2)}, u32[]{:S(2)}) %collective-permute-start.65) | collective-permute-done | bytes 8224 | tf_op jit(solution)/shard_map/ppermute | solution.py:24
  214.1 1.4 collective-permute-start.66
  216.2 1.6 collective-permute-done.66
  (297 shorter events, 68.1 us)
Async XLA Ops:
  0.7 54.0 %collective-permute-start.16 = (f32[1,8,64]{2,1,0:T(8,128)S(1)}, f32[1,8,64]{2,1,0:T(8,128)S(1)}, u32[]{:S(2)}, u32[]{:S(2)}) collective-permute-start(f32[1,8,64]{2,1,0:T(8,128)S(1)} %broadcast.203), channel_id=1, source_target_pairs={{2,0},{4,2},{6,4},{8,6},{10,8},{12,10},{14,12},{16,14},{18,16},{20... | collective-permute-start | bytes 6152 | tf_op jit(solution)/shard_map/ppermute | solution.py:27
  6.2 48.5 %collective-permute-start.17 = (f32[1,8,64]{2,1,0:T(8,128)S(1)}, f32[1,8,64]{2,1,0:T(8,128)S(1)}, u32[]{:S(2)}, u32[]{:S(2)}) collective-permute-start(f32[1,8,64]{2,1,0:T(8,128)S(1)} %broadcast.203), channel_id=1, source_target_pairs={{0,2},{2,4},{4,6},{6,8},{8,10},{10,12},{12,14},{14,16},{16,18},{18... | collective-permute-start | bytes 6152 | tf_op jit(solution)/shard_map/ppermute | solution.py:24
  6.2 13.9 %collective-permute-start.34 = (f32[1,4,16]{2,1,0:T(4,128)S(1)}, f32[1,4,16]{2,1,0:T(4,128)S(1)}, u32[]{:S(2)}, u32[]{:S(2)}) collective-permute-start(f32[1,4,16]{2,1,0:T(4,128)S(1)} %broadcast.212), channel_id=1, source_target_pairs={{2,0},{4,2},{6,4},{8,6},{10,8},{12,10},{14,12},{16,14},{18,16},{20... | collective-permute-start | bytes 776 | tf_op jit(solution)/shard_map/ppermute | solution.py:27
  10.6 11.1 %collective-permute-start.35 = (f32[1,4,16]{2,1,0:T(4,128)S(1)}, f32[1,4,16]{2,1,0:T(4,128)S(1)}, u32[]{:S(2)}, u32[]{:S(2)}) collective-permute-start(f32[1,4,16]{2,1,0:T(4,128)S(1)} %broadcast.212), channel_id=1, source_target_pairs={{0,2},{2,4},{4,6},{6,8},{8,10},{10,12},{12,14},{14,16},{16,18},{18... | collective-permute-start | bytes 776 | tf_op jit(solution)/shard_map/ppermute | solution.py:24
  11.3 5.8 %collective-permute-start.5 = (f32[1,16,128]{2,1,0:T(8,128)S(1)}, f32[1,16,128]{2,1,0:T(8,128)S(1)}, u32[]{:S(2)}, u32[]{:S(2)}) collective-permute-start(f32[1,16,128]{2,1,0:T(8,128)S(1)} %get-tuple-element.83), channel_id=1, source_target_pairs={{0,2},{2,4},{4,6},{6,8},{8,10},{10,12},{12,14},{14,16},{16,18},{18... | collective-permute-start | bytes 24584 | tf_op jit(solution)/shard_map/ppermute | solution.py:24
  20.1 8.8 %collective-permute-start = (f32[4,3,16,128]{3,2,1,0:T(8,128)S(1)}, f32[4,3,16,128]{3,2,1,0:T(8,128)S(1)}, u32[]{:S(2)}, u32[]{:S(2)}) collective-permute-start(f32[4,3,16,128]{3,2,1,0:T(8,128)S(1)} %get-tuple-element.44), channel_id=1, source_target_pairs={{0,2},{2,4},{4,6},{6,8},{8,10},{10,12},{12,14},{14,16},{16,18},{18... | collective-permute-start | bytes 294920 | tf_op jit(solution)/shard_map/ppermute | solution.py:24
  20.1 3.7 %collective-permute-start.6 = (f32[18,1,128]{2,1,0:T(1,128)S(1)}, f32[18,1,128]{2,1,0:T(1,128)S(1)}, u32[]{:S(2)}, u32[]{:S(2)}) collective-permute-start(f32[18,1,128]{2,1,0:T(1,128)S(1)} %get-tuple-element.71), channel_id=1, source_target_pairs={{1,0},{0,1},{3,2},{2,3},{5,4},{4,5},{7,6},{6,7},{9,8},{8,9},{11,10... | collective-permute-start | bytes 27656 | tf_op jit(solution)/shard_map/ppermute | solution.py:27
  21.7 5.5 %collective-permute-start.7 = (f32[18,1,128]{2,1,0:T(1,128)S(1)}, f32[18,1,128]{2,1,0:T(1,128)S(1)}, u32[]{:S(2)}, u32[]{:S(2)}) collective-permute-start(f32[18,1,128]{2,1,0:T(1,128)S(1)} %get-tuple-element.70), channel_id=1, source_target_pairs={{0,1},{1,0},{2,3},{3,2},{4,5},{5,4},{6,7},{7,6},{8,9},{9,8},{10,11... | collective-permute-start | bytes 27656 | tf_op jit(solution)/shard_map/ppermute | solution.py:24
  23.8 5.6 %collective-permute-start.1 = (f32[4,3,16,128]{3,2,1,0:T(8,128)S(1)}, f32[4,3,16,128]{3,2,1,0:T(8,128)S(1)}, u32[]{:S(2)}, u32[]{:S(2)}) collective-permute-start(f32[4,3,16,128]{3,2,1,0:T(8,128)S(1)} %get-tuple-element.45), channel_id=1, source_target_pairs={{2,0},{4,2},{6,4},{8,6},{10,8},{12,10},{14,12},{16,14},{18,16},{20... | collective-permute-start | bytes 294920 | tf_op jit(solution)/shard_map/ppermute | solution.py:27
  27.2 19.6 %collective-permute-start.28 = (f32[1,8,32]{1,2,0:T(8,128)S(1)}, f32[1,8,32]{1,2,0:T(8,128)S(1)}, u32[]{:S(2)}, u32[]{:S(2)}) collective-permute-start(f32[1,8,32]{1,2,0:T(8,128)S(1)} %broadcast.207), channel_id=1, source_target_pairs={{2,0},{4,2},{6,4},{8,6},{10,8},{12,10},{14,12},{16,14},{18,16},{20... | collective-permute-start | bytes 3080 | tf_op jit(solution)/shard_map/ppermute | solution.py:27
  29.5 5.4 %collective-permute-start.2 = (f32[4,22,3,128]{3,0,2,1:T(4,128)S(1)}, f32[4,22,3,128]{3,0,2,1:T(4,128)S(1)}, u32[]{:S(2)}, u32[]{:S(2)}) collective-permute-start(f32[4,22,3,128]{3,0,2,1:T(4,128)S(1)} %copy.568), channel_id=1, source_target_pairs={{0,1},{1,0},{2,3},{3,2},{4,5},{5,4},{6,7},{7,6},{8,9},{9,8},{10,11... | collective-permute-start | bytes 405512 | tf_op jit(solution)/shard_map/ppermute | solution.py:24
  31.1 5.2 %collective-permute-start.3 = (f32[4,22,3,128]{3,0,2,1:T(4,128)S(1)}, f32[4,22,3,128]{3,0,2,1:T(4,128)S(1)}, u32[]{:S(2)}, u32[]{:S(2)}) collective-permute-start(f32[4,22,3,128]{3,0,2,1:T(4,128)S(1)} %copy.569), channel_id=1, source_target_pairs={{1,0},{0,1},{3,2},{2,3},{5,4},{4,5},{7,6},{6,7},{9,8},{8,9},{11,10... | collective-permute-start | bytes 405512 | tf_op jit(solution)/shard_map/ppermute | solution.py:27
  34.9 11.9 %collective-permute-start.29 = (f32[1,8,32]{1,2,0:T(8,128)S(1)}, f32[1,8,32]{1,2,0:T(8,128)S(1)}, u32[]{:S(2)}, u32[]{:S(2)}) collective-permute-start(f32[1,8,32]{1,2,0:T(8,128)S(1)} %broadcast.207), channel_id=1, source_target_pairs={{0,2},{2,4},{4,6},{6,8},{8,10},{10,12},{12,14},{14,16},{16,18},{18... | collective-permute-start | bytes 3080 | tf_op jit(solution)/shard_map/ppermute | solution.py:24
  43.0 5.1 %collective-permute-start.8 = (f32[1,16,128]{2,1,0:T(8,128)S(1)}, f32[1,16,128]{2,1,0:T(8,128)S(1)}, u32[]{:S(2)}, u32[]{:S(2)}) collective-permute-start(f32[1,16,128]{2,1,0:T(8,128)S(1)} %get-tuple-element.81), channel_id=1, source_target_pairs={{2,0},{4,2},{6,4},{8,6},{10,8},{12,10},{14,12},{16,14},{18,16},{20... | collective-permute-start | bytes 24584 | tf_op jit(solution)/shard_map/ppermute | solution.py:27
  46.8 5.8 %collective-permute-start.9 = (f32[1,16,128]{2,1,0:T(8,128)S(1)}, f32[1,16,128]{2,1,0:T(8,128)S(1)}, u32[]{:S(2)}, u32[]{:S(2)}) collective-permute-start(f32[1,16,128]{2,1,0:T(8,128)S(1)} %get-tuple-element.80), channel_id=1, source_target_pairs={{0,2},{2,4},{4,6},{6,8},{8,10},{10,12},{12,14},{14,16},{16,18},{18... | collective-permute-start | bytes 24584 | tf_op jit(solution)/shard_map/ppermute | solution.py:24
  52.6 4.2 %collective-permute-start.10 = (f32[18,1,128]{2,1,0:T(1,128)S(1)}, f32[18,1,128]{2,1,0:T(1,128)S(1)}, u32[]{:S(2)}, u32[]{:S(2)}) collective-permute-start(f32[18,1,128]{2,1,0:T(1,128)S(1)} %get-tuple-element.69), channel_id=1, source_target_pairs={{1,0},{0,1},{3,2},{2,3},{5,4},{4,5},{7,6},{6,7},{9,8},{8,9},{11,10... | collective-permute-start | bytes 27656 | tf_op jit(solution)/shard_map/ppermute | solution.py:27
  54.0 3.7 %collective-permute-start.11 = (f32[18,1,128]{2,1,0:T(1,128)S(1)}, f32[18,1,128]{2,1,0:T(1,128)S(1)}, u32[]{:S(2)}, u32[]{:S(2)}) collective-permute-start(f32[18,1,128]{2,1,0:T(1,128)S(1)} %get-tuple-element.68), channel_id=1, source_target_pairs={{0,1},{1,0},{2,3},{3,2},{4,5},{5,4},{6,7},{7,6},{8,9},{9,8},{10,11... | collective-permute-start | bytes 27656 | tf_op jit(solution)/shard_map/ppermute | solution.py:24
  54.7 3.9 %collective-permute-start.18 = (f32[10,1,64]{2,1,0:T(1,128)S(1)}, f32[10,1,64]{2,1,0:T(1,128)S(1)}, u32[]{:S(2)}, u32[]{:S(2)}) collective-permute-start(f32[10,1,64]{2,1,0:T(1,128)S(1)} %get-tuple-element.143), channel_id=1, source_target_pairs={{1,0},{0,1},{3,2},{2,3},{5,4},{4,5},{7,6},{6,7},{9,8},{8,9},{11,10... | collective-permute-start | bytes 7688 | tf_op jit(solution)/shard_map/ppermute | solution.py:27
  56.1 3.6 %collective-permute-start.19 = (f32[10,1,64]{2,1,0:T(1,128)S(1)}, f32[10,1,64]{2,1,0:T(1,128)S(1)}, u32[]{:S(2)}, u32[]{:S(2)}) collective-permute-start(f32[10,1,64]{2,1,0:T(1,128)S(1)} %get-tuple-element.142), channel_id=1, source_target_pairs={{0,1},{1,0},{2,3},{3,2},{4,5},{5,4},{6,7},{7,6},{8,9},{9,8},{10,11... | collective-permute-start | bytes 7688 | tf_op jit(solution)/shard_map/ppermute | solution.py:24
  58.1 5.8 %collective-permute-start.13 = (f32[1,16,128]{2,1,0:T(8,128)S(1)}, f32[1,16,128]{2,1,0:T(8,128)S(1)}, u32[]{:S(2)}, u32[]{:S(2)}) collective-permute-start(f32[1,16,128]{2,1,0:T(8,128)S(1)} %get-tuple-element.78), channel_id=1, source_target_pairs={{0,2},{2,4},{4,6},{6,8},{8,10},{10,12},{12,14},{14,16},{16,18},{18... | collective-permute-start | bytes 24584 | tf_op jit(solution)/shard_map/ppermute | solution.py:24
  64.0 3.7 %collective-permute-start.14 = (f32[18,1,128]{2,1,0:T(1,128)S(1)}, f32[18,1,128]{2,1,0:T(1,128)S(1)}, u32[]{:S(2)}, u32[]{:S(2)}) collective-permute-start(f32[18,1,128]{2,1,0:T(1,128)S(1)} %get-tuple-element.67), channel_id=1, source_target_pairs={{1,0},{0,1},{3,2},{2,3},{5,4},{4,5},{7,6},{6,7},{9,8},{8,9},{11,10... | collective-permute-start | bytes 27656 | tf_op jit(solution)/shard_map/ppermute | solution.py:27
  64.7 3.7 %collective-permute-start.15 = (f32[18,1,128]{2,1,0:T(1,128)S(1)}, f32[18,1,128]{2,1,0:T(1,128)S(1)}, u32[]{:S(2)}, u32[]{:S(2)}) collective-permute-start(f32[18,1,128]{2,1,0:T(1,128)S(1)} %get-tuple-element.66), channel_id=1, source_target_pairs={{0,1},{1,0},{2,3},{3,2},{4,5},{5,4},{6,7},{7,6},{8,9},{9,8},{10,11... | collective-permute-start | bytes 27656 | tf_op jit(solution)/shard_map/ppermute | solution.py:24
  82.8 6.0 %collective-permute-start.21 = (f32[1,8,64]{2,1,0:T(8,128)S(1)}, f32[1,8,64]{2,1,0:T(8,128)S(1)}, u32[]{:S(2)}, u32[]{:S(2)}) collective-permute-start(f32[1,8,64]{2,1,0:T(8,128)S(1)} %get-tuple-element.150), channel_id=1, source_target_pairs={{0,2},{2,4},{4,6},{6,8},{8,10},{10,12},{12,14},{14,16},{16,18},{18... | collective-permute-start | bytes 6152 | tf_op jit(solution)/shard_map/ppermute | solution.py:24
  88.8 3.7 %collective-permute-start.22 = (f32[10,1,64]{2,1,0:T(1,128)S(1)}, f32[10,1,64]{2,1,0:T(1,128)S(1)}, u32[]{:S(2)}, u32[]{:S(2)}) collective-permute-start(f32[10,1,64]{2,1,0:T(1,128)S(1)} %get-tuple-element.141), channel_id=1, source_target_pairs={{1,0},{0,1},{3,2},{2,3},{5,4},{4,5},{7,6},{6,7},{9,8},{8,9},{11,10... | collective-permute-start | bytes 7688 | tf_op jit(solution)/shard_map/ppermute | solution.py:27
  94.1 5.8 %collective-permute-start.25 = (f32[1,8,64]{2,1,0:T(8,128)S(1)}, f32[1,8,64]{2,1,0:T(8,128)S(1)}, u32[]{:S(2)}, u32[]{:S(2)}) collective-permute-start(f32[1,8,64]{2,1,0:T(8,128)S(1)} %get-tuple-element.148), channel_id=1, source_target_pairs={{0,2},{2,4},{4,6},{6,8},{8,10},{10,12},{12,14},{14,16},{16,18},{18... | collective-permute-start | bytes 6152 | tf_op jit(solution)/shard_map/ppermute | solution.py:24
  99.9 3.7 %collective-permute-start.26 = (f32[10,1,64]{2,1,0:T(1,128)S(1)}, f32[10,1,64]{2,1,0:T(1,128)S(1)}, u32[]{:S(2)}, u32[]{:S(2)}) collective-permute-start(f32[10,1,64]{2,1,0:T(1,128)S(1)} %get-tuple-element.139), channel_id=1, source_target_pairs={{1,0},{0,1},{3,2},{2,3},{5,4},{4,5},{7,6},{6,7},{9,8},{8,9},{11,10... | collective-permute-start | bytes 7688 | tf_op jit(solution)/shard_map/ppermute | solution.py:27
  110.4 5.9 %collective-permute-start.31 = (f32[1,8,32]{1,2,0:T(8,128)S(1)}, f32[1,8,32]{1,2,0:T(8,128)S(1)}, u32[]{:S(2)}, u32[]{:S(2)}) collective-permute-start(f32[1,8,32]{1,2,0:T(8,128)S(1)} %get-tuple-element.112), channel_id=1, source_target_pairs={{0,2},{2,4},{4,6},{6,8},{8,10},{10,12},{12,14},{14,16},{16,18},{18... | collective-permute-start | bytes 3080 | tf_op jit(solution)/shard_map/ppermute | solution.py:24
  117.4 5.9 %collective-permute-start.33 = (f32[1,8,32]{1,2,0:T(8,128)S(1)}, f32[1,8,32]{1,2,0:T(8,128)S(1)}, u32[]{:S(2)}, u32[]{:S(2)}) collective-permute-start(f32[1,8,32]{1,2,0:T(8,128)S(1)} %get-tuple-element.110), channel_id=1, source_target_pairs={{0,2},{2,4},{4,6},{6,8},{8,10},{10,12},{12,14},{14,16},{16,18},{18... | collective-permute-start | bytes 3080 | tf_op jit(solution)/shard_map/ppermute | solution.py:24
  124.8 5.8 %collective-permute-start.37 = (f32[1,4,16]{2,1,0:T(4,128)S(1)}, f32[1,4,16]{2,1,0:T(4,128)S(1)}, u32[]{:S(2)}, u32[]{:S(2)}) collective-permute-start(f32[1,4,16]{2,1,0:T(4,128)S(1)} %get-tuple-element.178), channel_id=1, source_target_pairs={{0,2},{2,4},{4,6},{6,8},{8,10},{10,12},{12,14},{14,16},{16,18},{18... | collective-permute-start | bytes 776 | tf_op jit(solution)/shard_map/ppermute | solution.py:24
  130.8 5.8 %collective-permute-start.39 = (f32[1,4,16]{2,1,0:T(4,128)S(1)}, f32[1,4,16]{2,1,0:T(4,128)S(1)}, u32[]{:S(2)}, u32[]{:S(2)}) collective-permute-start(f32[1,4,16]{2,1,0:T(4,128)S(1)} %get-tuple-element.176), channel_id=1, source_target_pairs={{0,2},{2,4},{4,6},{6,8},{8,10},{10,12},{12,14},{14,16},{16,18},{18... | collective-permute-start | bytes 776 | tf_op jit(solution)/shard_map/ppermute | solution.py:24
  136.9 5.8 %collective-permute-start.41 = (f32[1,4,16]{2,1,0:T(4,128)S(1)}, f32[1,4,16]{2,1,0:T(4,128)S(1)}, u32[]{:S(2)}, u32[]{:S(2)}) collective-permute-start(f32[1,4,16]{2,1,0:T(4,128)S(1)} %get-tuple-element.174), channel_id=1, source_target_pairs={{0,2},{2,4},{4,6},{6,8},{8,10},{10,12},{12,14},{14,16},{16,18},{18... | collective-permute-start | bytes 776 | tf_op jit(solution)/shard_map/ppermute | solution.py:24
  142.9 5.8 %collective-permute-start.43 = (f32[1,4,16]{2,1,0:T(4,128)S(1)}, f32[1,4,16]{2,1,0:T(4,128)S(1)}, u32[]{:S(2)}, u32[]{:S(2)}) collective-permute-start(f32[1,4,16]{2,1,0:T(4,128)S(1)} %get-tuple-element.172), channel_id=1, source_target_pairs={{0,2},{2,4},{4,6},{6,8},{8,10},{10,12},{12,14},{14,16},{16,18},{18... | collective-permute-start | bytes 776 | tf_op jit(solution)/shard_map/ppermute | solution.py:24
  149.1 5.9 %collective-permute-start.45 = (f32[1,8,32]{1,2,0:T(8,128)S(1)}, f32[1,8,32]{1,2,0:T(8,128)S(1)}, u32[]{:S(2)}, u32[]{:S(2)}) collective-permute-start(f32[1,8,32]{1,2,0:T(8,128)S(1)} %get-tuple-element.108), channel_id=1, source_target_pairs={{0,2},{2,4},{4,6},{6,8},{8,10},{10,12},{12,14},{14,16},{16,18},{18... | collective-permute-start | bytes 3080 | tf_op jit(solution)/shard_map/ppermute | solution.py:24
  156.1 5.9 %collective-permute-start.47 = (f32[1,8,32]{1,2,0:T(8,128)S(1)}, f32[1,8,32]{1,2,0:T(8,128)S(1)}, u32[]{:S(2)}, u32[]{:S(2)}) collective-permute-start(f32[1,8,32]{1,2,0:T(8,128)S(1)} %get-tuple-element.106), channel_id=1, source_target_pairs={{0,2},{2,4},{4,6},{6,8},{8,10},{10,12},{12,14},{14,16},{16,18},{18... | collective-permute-start | bytes 3080 | tf_op jit(solution)/shard_map/ppermute | solution.py:24
  163.6 5.8 %collective-permute-start.49 = (f32[1,8,64]{2,1,0:T(8,128)S(1)}, f32[1,8,64]{2,1,0:T(8,128)S(1)}, u32[]{:S(2)}, u32[]{:S(2)}) collective-permute-start(f32[1,8,64]{2,1,0:T(8,128)S(1)} %get-tuple-element.146), channel_id=1, source_target_pairs={{0,2},{2,4},{4,6},{6,8},{8,10},{10,12},{12,14},{14,16},{16,18},{18... | collective-permute-start | bytes 6152 | tf_op jit(solution)/shard_map/ppermute | solution.py:24
  169.4 3.7 %collective-permute-start.50 = (f32[10,1,64]{2,1,0:T(1,128)S(1)}, f32[10,1,64]{2,1,0:T(1,128)S(1)}, u32[]{:S(2)}, u32[]{:S(2)}) collective-permute-start(f32[10,1,64]{2,1,0:T(1,128)S(1)} %get-tuple-element.117), channel_id=1, source_target_pairs={{1,0},{0,1},{3,2},{2,3},{5,4},{4,5},{7,6},{6,7},{9,8},{8,9},{11,10... | collective-permute-start | bytes 7688 | tf_op jit(solution)/shard_map/ppermute | solution.py:27
  174.8 5.8 %collective-permute-start.53 = (f32[1,8,64]{2,1,0:T(8,128)S(1)}, f32[1,8,64]{2,1,0:T(8,128)S(1)}, u32[]{:S(2)}, u32[]{:S(2)}) collective-permute-start(f32[1,8,64]{2,1,0:T(8,128)S(1)} %get-tuple-element.144), channel_id=1, source_target_pairs={{0,2},{2,4},{4,6},{6,8},{8,10},{10,12},{12,14},{14,16},{16,18},{18... | collective-permute-start | bytes 6152 | tf_op jit(solution)/shard_map/ppermute | solution.py:24
  180.6 3.7 %collective-permute-start.54 = (f32[10,1,64]{2,1,0:T(1,128)S(1)}, f32[10,1,64]{2,1,0:T(1,128)S(1)}, u32[]{:S(2)}, u32[]{:S(2)}) collective-permute-start(f32[10,1,64]{2,1,0:T(1,128)S(1)} %get-tuple-element.115), channel_id=1, source_target_pairs={{1,0},{0,1},{3,2},{2,3},{5,4},{4,5},{7,6},{6,7},{9,8},{8,9},{11,10... | collective-permute-start | bytes 7688 | tf_op jit(solution)/shard_map/ppermute | solution.py:27
  181.3 3.6 %collective-permute-start.55 = (f32[10,1,64]{2,1,0:T(1,128)S(1)}, f32[10,1,64]{2,1,0:T(1,128)S(1)}, u32[]{:S(2)}, u32[]{:S(2)}) collective-permute-start(f32[10,1,64]{2,1,0:T(1,128)S(1)} %get-tuple-element.114), channel_id=1, source_target_pairs={{0,1},{1,0},{2,3},{3,2},{4,5},{5,4},{6,7},{7,6},{8,9},{9,8},{10,11... | collective-permute-start | bytes 7688 | tf_op jit(solution)/shard_map/ppermute | solution.py:24
  186.1 5.8 %collective-permute-start.57 = (f32[1,16,128]{2,1,0:T(8,128)S(1)}, f32[1,16,128]{2,1,0:T(8,128)S(1)}, u32[]{:S(2)}, u32[]{:S(2)}) collective-permute-start(f32[1,16,128]{2,1,0:T(8,128)S(1)} %get-tuple-element.76), channel_id=1, source_target_pairs={{0,2},{2,4},{4,6},{6,8},{8,10},{10,12},{12,14},{14,16},{16,18},{18... | collective-permute-start | bytes 24584 | tf_op jit(solution)/shard_map/ppermute | solution.py:24
  192.0 3.7 %collective-permute-start.58 = (f32[18,1,128]{2,1,0:T(1,128)S(1)}, f32[18,1,128]{2,1,0:T(1,128)S(1)}, u32[]{:S(2)}, u32[]{:S(2)}) collective-permute-start(f32[18,1,128]{2,1,0:T(1,128)S(1)} %get-tuple-element.65), channel_id=1, source_target_pairs={{1,0},{0,1},{3,2},{2,3},{5,4},{4,5},{7,6},{6,7},{9,8},{8,9},{11,10... | collective-permute-start | bytes 27656 | tf_op jit(solution)/shard_map/ppermute | solution.py:27
  193.4 3.7 %collective-permute-start.59 = (f32[18,1,128]{2,1,0:T(1,128)S(1)}, f32[18,1,128]{2,1,0:T(1,128)S(1)}, u32[]{:S(2)}, u32[]{:S(2)}) collective-permute-start(f32[18,1,128]{2,1,0:T(1,128)S(1)} %get-tuple-element.64), channel_id=1, source_target_pairs={{0,1},{1,0},{2,3},{3,2},{4,5},{5,4},{6,7},{7,6},{8,9},{9,8},{10,11... | collective-permute-start | bytes 27656 | tf_op jit(solution)/shard_map/ppermute | solution.py:24
  197.5 5.8 %collective-permute-start.61 = (f32[1,16,128]{2,1,0:T(8,128)S(1)}, f32[1,16,128]{2,1,0:T(8,128)S(1)}, u32[]{:S(2)}, u32[]{:S(2)}) collective-permute-start(f32[1,16,128]{2,1,0:T(8,128)S(1)} %get-tuple-element.74), channel_id=1, source_target_pairs={{0,2},{2,4},{4,6},{6,8},{8,10},{10,12},{12,14},{14,16},{16,18},{18... | collective-permute-start | bytes 24584 | tf_op jit(solution)/shard_map/ppermute | solution.py:24
  203.4 3.7 %collective-permute-start.62 = (f32[18,1,128]{2,1,0:T(1,128)S(1)}, f32[18,1,128]{2,1,0:T(1,128)S(1)}, u32[]{:S(2)}, u32[]{:S(2)}) collective-permute-start(f32[18,1,128]{2,1,0:T(1,128)S(1)} %get-tuple-element.63), channel_id=1, source_target_pairs={{1,0},{0,1},{3,2},{2,3},{5,4},{4,5},{7,6},{6,7},{9,8},{8,9},{11,10... | collective-permute-start | bytes 27656 | tf_op jit(solution)/shard_map/ppermute | solution.py:27
  204.1 3.7 %collective-permute-start.63 = (f32[18,1,128]{2,1,0:T(1,128)S(1)}, f32[18,1,128]{2,1,0:T(1,128)S(1)}, u32[]{:S(2)}, u32[]{:S(2)}) collective-permute-start(f32[18,1,128]{2,1,0:T(1,128)S(1)} %get-tuple-element.62), channel_id=1, source_target_pairs={{0,1},{1,0},{2,3},{3,2},{4,5},{5,4},{6,7},{7,6},{8,9},{9,8},{10,11... | collective-permute-start | bytes 27656 | tf_op jit(solution)/shard_map/ppermute | solution.py:24
  208.3 5.8 %collective-permute-start.65 = (f32[1,16,128]{2,1,0:T(8,128)S(1)}, f32[1,16,128]{2,1,0:T(8,128)S(1)}, u32[]{:S(2)}, u32[]{:S(2)}) collective-permute-start(f32[1,16,128]{2,1,0:T(8,128)S(1)} %get-tuple-element.72), channel_id=1, source_target_pairs={{0,2},{2,4},{4,6},{6,8},{8,10},{10,12},{12,14},{14,16},{16,18},{18... | collective-permute-start | bytes 24584 | tf_op jit(solution)/shard_map/ppermute | solution.py:24
  214.1 3.7 %collective-permute-start.66 = (f32[18,1,128]{2,1,0:T(1,128)S(1)}, f32[18,1,128]{2,1,0:T(1,128)S(1)}, u32[]{:S(2)}, u32[]{:S(2)}) collective-permute-start(f32[18,1,128]{2,1,0:T(1,128)S(1)} %get-tuple-element.61), channel_id=1, source_target_pairs={{1,0},{0,1},{3,2},{2,3},{5,4},{4,5},{7,6},{6,7},{9,8},{8,9},{11,10... | collective-permute-start | bytes 27656 | tf_op jit(solution)/shard_map/ppermute | solution.py:27
  215.5 3.7 %collective-permute-start.67 = (f32[18,1,128]{2,1,0:T(1,128)S(1)}, f32[18,1,128]{2,1,0:T(1,128)S(1)}, u32[]{:S(2)}, u32[]{:S(2)}) collective-permute-start(f32[18,1,128]{2,1,0:T(1,128)S(1)} %get-tuple-element.60), channel_id=1, source_target_pairs={{0,1},{1,0},{2,3},{3,2},{4,5},{5,4},{6,7},{7,6},{8,9},{9,8},{10,11... | collective-permute-start | bytes 27656 | tf_op jit(solution)/shard_map/ppermute | solution.py:24
  (23 other events, 78.8 us)
where the time goes:
time: 221 us; the launch traced here: 220 us
  waiting for transfers between devices  122 us (55%)
  starting transfers between devices  54.4 us (25%)
  local copies, waits for them, and re-layouts  20.3 us (9%)
  other arithmetic  17.7 us (8%)
  blocking collectives  4.36 us (2%)
    ppermute x34, waiting for transfers between devices, with_halo(): lax.ppermute(lax.slice_in_dim(block, block.shape[dim] - width, None, axis...  91.8 us
    ppermute x34, starting transfers between devices, with_halo(): lax.ppermute(lax.slice_in_dim(block, 0, width, axis=dim), axis, backward)  34.9 us
    ppermute x34, waiting for transfers between devices, with_halo(): lax.ppermute(lax.slice_in_dim(block, 0, width, axis=dim), axis, backward)  30.1 us
    ppermute x34, starting transfers between devices, with_halo(): lax.ppermute(lax.slice_in_dim(block, block.shape[dim] - width, None, axis...  19.5 us
    reshape x3, local copies, waits for them, and re-layouts, coarsen(): values.reshape(values.shape[0] // 2, 2, values.shape[1] // 2, 2, values.s...  11 us
  transfers between devices with their start and end apart: 68, of which 57 were waited for; matrix products, arithmetic and copies ran while one was open for 6% of the time, Pallas kernels for 0%

commit v1 on v0

v1 whole, which is shorter than its diff:
```python
import functools

import jax
import jax.numpy as jnp
from jax import lax
from jax.experimental import pallas as pl
from jax.experimental.pallas import tpu as pltpu
from jax.sharding import PartitionSpec as P

MESH = pl.DeviceIdType.MESH
F32 = jnp.float32
STEP = 0.1
WEIGHT = 0.8 / 12.0
KEEP = 0.2
OFF = 3
REACH = 4


def loop(low, high, body):
    def step(index, carry):
        body(index)
        return carry

    lax.fori_loop(low, high, step, 0)


def kernel(
    nx, ny, vel_in, pre_in, turb_in, ground_in, vel_out, pre_out,
    W, WLO, WHI, WSL, WSH, D, DLO, DHI, DSL, DSH, PA, PLO, PHI, PSL, PSH,
    PB, PC, CLO, CHI, CSL, CSH, F, FLO, FHI, FSL, FSH, T, S, tmp, tmp2, turb, ground,
    G1, F1, P1A, P1B, G2, F2, P2A, P2B, F3, P3A, P3B, E1, E0,
    load_sem, send_sem, recv_sem,
):
    me_x, me_y = lax.axis_index("gx"), lax.axis_index("gy")
    own_x, own_y, nz = pre_out.shape
    side = (own_y // 8 + 1) * 8
    rows = own_x + 2 * OFF

    loads = [
        pltpu.make_async_copy(vel_in, W.at[:, OFF : OFF + own_x, 0:own_y], load_sem.at[0]),
        pltpu.make_async_copy(pre_in, PA.at[OFF : OFF + own_x, 0:own_y], load_sem.at[1]),
        pltpu.make_async_copy(turb_in, turb, load_sem.at[2]),
        pltpu.make_async_copy(ground_in, ground, load_sem.at[3]),
    ]
    for load in loads:
        load.start()

    def device(dx, dy):
        return (lax.rem(me_x + dx + nx, nx), lax.rem(me_y + dy + ny, ny))

    friends = [(dx, 0) for dx in range(-REACH, REACH + 1) if dx != 0]
    friends += [(dx, dy) for dx in (-1, 0, 1) for dy in range(1, ny)]
    barrier = pltpu.get_barrier_semaphore()
    for dx, dy in friends:
        pl.semaphore_signal(barrier, inc=1, device_id=device(dx, dy), device_id_type=MESH)

    used = [0]

    def remote(src, dst, where):
        slot = used[0]
        used[0] += 1
        copy = pltpu.make_async_remote_copy(
            src_ref=src, dst_ref=dst, send_sem=send_sem.at[slot], recv_sem=recv_sem.at[slot],
            device_id=where, device_id_type=MESH,
        )
        copy.start()
        return copy

    def spans(dx, width, base):
        if dx == 0:
            return pl.ds(base, own_x), pl.ds(base, own_x)
        if dx == 1:
            return pl.ds(base + own_x - width, width), pl.ds(base - width, width)
        return pl.ds(base, width), pl.ds(base + own_x, width)

    def pick(ref, span, lead):
        return ref.at[:, span] if lead else ref.at[span]

    def send_x(M, width, lead=False):
        copies = []
        for dx in (1, -1):
            src, dst = spans(dx, width, OFF)
            a = M.at[:, src, 0:own_y] if lead else M.at[src, 0:own_y]
            b = M.at[:, dst, 0:own_y] if lead else M.at[dst, 0:own_y]
            copies.append(remote(a, b, device(dx, 0)))
        return copies

    def send_y(M, LO, HI, SL, SH, width, lead=False):
        if lead:
            SL[...] = M[:, OFF : OFF + own_x, own_y - width : own_y, :]
            SH[...] = M[:, OFF : OFF + own_x, 0:width, :]
        else:
            SL[...] = M[OFF : OFF + own_x, own_y - width : own_y, :]
            SH[...] = M[OFF : OFF + own_x, 0:width, :]
        copies = []
        for dx in (0, 1, -1):
            src, dst = spans(dx, width, width)
            if dx == 0:
                src = pl.ds(0, own_x)
            elif dx == 1:
                src = pl.ds(own_x - width, width)
            else:
                src = pl.ds(0, width)
            copies.append(remote(pick(SL, src, lead), pick(LO, dst, lead), device(dx, 1)))
            copies.append(remote(pick(SH, src, lead), pick(HI, dst, lead), device(dx, -1)))
        return copies

    def finish(copies):
        for copy in copies:
            copy.wait()

    def place(M, LO, HI, width, lead=False):
        lo, hi = OFF - width, OFF + own_x + width
        if lead:
            M[:, lo:hi, own_y : own_y + width, :] = HI[...]
            M[:, lo:hi, side - width : side, :] = LO[...]
        else:
            M[lo:hi, own_y : own_y + width, :] = HI[...]
            M[lo:hi, side - width : side, :] = LO[...]

    def lane_of(count):
        return lax.broadcasted_iota(jnp.int32, (count, nz), 1)

    def roll(v, shift, axis):
        return pltpu.roll(v, shift % v.shape[axis], axis)

    lane16 = lane_of(own_y)
    loads[2].wait()
    loads[3].wait()
    for x in range(own_x):
        low = jnp.where(lane16 == 0, roll(ground[...], -x, 1), 0.0)
        D[OFF + x, 0:own_y, :] = 2.0 * turb[x].astype(F32) + low
    loads[0].wait()
    loads[1].wait()
    pl.semaphore_wait(barrier, len(friends))
    w_copies = send_y(W, WLO, WHI, WSL, WSH, 3, True) + send_x(W, 3, True)
    d_copies = send_y(D, DLO, DHI, DSL, DSH, 1) + send_x(D, 1)
    p_copies = send_y(PA, PLO, PHI, PSL, PSH, 3) + send_x(PA, 3)
    finish(w_copies)
    place(W, WLO, WHI, 3, True)
    finish(d_copies)
    place(D, DLO, DHI, 1)

    lane = lane_of(side)
    first, last = lane == 0, lane == nz - 1

    def up0(v):
        return jnp.where(last, 0.0, roll(v, -1, 1))

    def down0(v):
        return jnp.where(first, 0.0, roll(v, 1, 1))

    def stress_row(r):
        v = [W[a, r] for a in range(3)]
        gx = [0.5 * (W[a, r + 1] - W[a, r - 1]) for a in range(3)]
        gy = [0.5 * (roll(v[a], -1, 0) - roll(v[a], 1, 0)) for a in range(3)]
        gz = [up0(v[a]) - down0(v[a]) for a in range(3)]
        e01, e02, e12 = gx[1] + gy[0], gx[2] + gz[0], gy[2] + gz[1]
        q = 2.0 * (gx[0] * gx[0] + gy[1] * gy[1] + gz[2] * gz[2]) + e01 * e01 + e02 * e02 + e12 * e12
        visc = 0.03 * jnp.sqrt(q)
        twice = visc + visc
        t00, t11, t22 = twice * gx[0], twice * gy[1], twice * gz[2]
        t01, t02, t12 = visc * e01, visc * e02, visc * e12
        flat = v[0] * v[0] + v[1] * v[1]
        ghost = 0.03 * jnp.sqrt(2.0 * v[2] * v[2] + flat)
        ghosts = [ghost * v[0], ghost * v[1], (ghost + ghost) * v[2]]
        T[0, r] = t00
        T[1, r] = t01
        T[2, r] = t02
        drag = D[r] * jnp.sqrt(flat)
        for a, (ty, tz) in enumerate(((t01, t02), (t11, t12), (t12, t22))):
            change = 0.5 * (roll(ty, -1, 0) - roll(ty, 1, 0))
            change += jnp.where(last, -ghosts[a], roll(tz, -1, 1)) - jnp.where(first, ghosts[a], roll(tz, 1, 1))
            change -= v[0] * gx[a] + v[1] * gy[a] + v[2] * gz[a]
            if a < 2:
                change -= drag * v[a]
            if a == 0:
                change += 1.0
            S[a, r] = v[a] + STEP * change

    loop(1, rows - 1, stress_row)

    def star_row(r):
        for a in range(3):
            S[a, r] = S[a, r] + (0.5 * STEP) * (T[a, r + 1] - T[a, r - 1])

    loop(2, rows - 2, star_row)

    def source_row(r):
        s1, s2 = S[1, r], S[2, r]
        flat = 0.5 * (S[0, r + 1] - S[0, r - 1] + roll(s1, -1, 0) - roll(s1, 1, 0))
        F[r] = (flat + up0(s2) - down0(s2)) / STEP

    loop(OFF, OFF + own_x, source_row)
    f_copies = send_y(F, FLO, FHI, FSL, FSH, 2) + send_x(F, 2)
    finish(p_copies)
    place(PA, PLO, PHI, 3)
    finish(f_copies)
    place(F, FLO, FHI, 2)

    def stencil(src, r, sy, sz):
        p = src[r]
        lanes = lane_of(p.shape[0])
        z = jnp.where(lanes >= nz - sz, p, roll(p, -sz, 1)) + jnp.where(lanes < sz, p, roll(p, sz, 1))
        s = src[r + 1] + src[r - 1] + roll(p, -sy, 0) + roll(p, sy, 0)
        return p, s + 4.0 * z

    def sweep(src, dst, f, low, high, sy, sz):
        def body(r):
            p, around = stencil(src, r, sy, sz)
            dst[r] = KEEP * p + WEIGHT * (around - f[r])

        loop(low, high, body)

    def residual(src, f, r, sy, sz):
        p, around = stencil(src, r, sy, sz)
        return f[r] - (around - 12.0 * p)

    def pair(v, stride, axis):
        at = lax.broadcasted_iota(jnp.int32, v.shape, axis)
        even = (at // stride) % 2 == 0
        return v + jnp.where(even, roll(v, -stride, axis), roll(v, stride, axis))

    def spread(v, stride, bit):
        at = (lane_of(v.shape[0]) // stride) % 2
        return jnp.where(at == bit, v, roll(v, stride if bit == 0 else -stride, 1))

    sweep(PA, PB, F, 1, rows - 1, 1, 1)
    sweep(PB, PA, F, 2, rows - 2, 1, 1)
    PC[OFF : OFF + own_x, 0:own_y, :] = PA[OFF : OFF + own_x, 0:own_y, :]

    half = own_x // 2
    y1 = own_y // 2

    def fine_residual(i):
        r = OFF + 2 * i
        v = residual(PA, F, r, 1, 1) + residual(PA, F, r + 1, 1, 1)
        tmp[i] = pair(v[0:own_y], 1, 1)

    loop(0, half, fine_residual)
    packed = half // 2
    lane8 = lane_of(y1)
    for i in range(packed):
        parts = []
        for x in (2 * i, 2 * i + 1):
            parts.append(0.5 * (tmp[x, pl.ds(0, y1, 2), :] + tmp[x, pl.ds(1, y1, 2), :]))
        G1[0, 3 + i] = jnp.where(lane8 % 2 == 0, parts[0], parts[1])
    g_copies = []
    for dx in (1, -1, 0):
        for dy in range(ny):
            if dx == 0 and dy == 0:
                continue
            if dx == 0:
                src, dst = pl.ds(3, packed), pl.ds(3, packed)
            elif dx == 1:
                src, dst = pl.ds(packed, 3), pl.ds(0, 3)
            else:
                src, dst = pl.ds(3, 3), pl.ds(3 + packed, 3)
            g_copies.append(remote(G1.at[0, src], G1.at[(ny - dy) % ny, dst], device(dx, dy)))
    c_copies = send_y(PC, CLO, CHI, CSL, CSH, 3) + send_x(PC, 3)
    finish(g_copies)
    rows1 = 2 * (packed + 6)
    for k in range(ny):
        for j in range(packed + 6):
            v = G1[k, j]
            for bit in (0, 1):
                f = spread(v, 1, bit)
                F1[2 * j + bit, k * y1 : (k + 1) * y1, :] = f
                P1A[2 * j + bit, k * y1 : (k + 1) * y1, :] = -WEIGHT * f
    sweep(P1A, P1B, F1, 1, rows1 - 1, 1, 2)
    quarter = half // 2
    y2 = ny * y1 // 2
    lane2 = lane_of(y2)
    gathered = None
    for i in range(quarter):
        r = 6 + 2 * i
        tmp2[i] = pair(residual(P1B, F1, r, 1, 2) + residual(P1B, F1, r + 1, 1, 2), 2, 1)
        v = 0.5 * (tmp2[i, pl.ds(0, y2, 2), :] + tmp2[i, pl.ds(1, y2, 2), :])
        gathered = v if gathered is None else jnp.where(lane2 % 4 == i, v, gathered)
    G2[REACH] = gathered
    finish([remote(G2.at[REACH], G2.at[REACH - dx], device(dx, 0)) for dx, dy in friends if dy == 0])
    for s in range(2 * REACH + 1):
        v = G2[s]
        for b0 in (0, 1):
            u = spread(v, 1, b0)
            for b1 in (0, 1):
                f = spread(u, 2, b1)
                F2[4 * s + 2 * b1 + b0] = f
                P2A[4 * s + 2 * b1 + b0] = -WEIGHT * f
    rows2 = 4 * (2 * REACH + 1)
    sweep(P2A, P2B, F2, 1, rows2 - 1, 1, 4)

    def coarse_source(i):
        v = residual(P2B, F2, 2 * i, 1, 4) + residual(P2B, F2, 2 * i + 1, 1, 4)
        f = 0.5 * pair(pair(v, 4, 1), 1, 0)
        F3[i] = f
        P3A[i] = -WEIGHT * f

    loop(1, rows2 // 2 - 1, coarse_source)
    sweep(P3A, P3B, F3, 2, 16, 2, 8)
    sweep(P3B, P3A, F3, 3, 15, 2, 8)
    sweep(P3A, P3B, F3, 4, 14, 2, 8)

    def line_row(r):
        mean = jnp.mean(residual(P3B, F3, r, 2, 8), axis=0, keepdims=True)
        v = P3B[r] - WEIGHT * mean
        P2B[2 * r] = P2B[2 * r] + v
        P2B[2 * r + 1] = P2B[2 * r + 1] + v

    loop(6, 12, line_row)
    sweep(P2B, P2A, F2, 13, 23, 1, 4)

    def second_row(m):
        p, around = stencil(P2A, m, 1, 4)
        v = KEEP * p + WEIGHT * (around - F2[m])
        E1[m - 14, pl.ds(0, y2, 2), :] = v
        E1[m - 14, pl.ds(1, y2, 2), :] = v
        e = E1[m - 14]
        r = 2 * (m - 13)
        P1B[r] = P1B[r] + e
        P1B[r + 1] = P1B[r + 1] + e

    for m in range(14, 22):
        second_row(m)
    sweep(P1B, P1A, F1, 3, 17, 1, 2)
    sweep(P1A, P1B, F1, 4, 16, 1, 2)
    finish(c_copies)
    place(PC, CLO, CHI, 3)
    full1 = ny * y1
    for m in range(4, 16):
        e = m - 4
        for shift in (0, 1):
            E0[e, pl.ds(shift, y1, 2), :] = P1B[m, 0:y1, :]
            E0[e, pl.ds(own_y + shift, 2, 2), :] = P1B[m, y1 : y1 + 2, :]
            E0[e, pl.ds(own_y + 4 + shift, 2, 2), :] = P1B[m, full1 - 2 : full1, :]
        for r in (2 * m - 9, 2 * m - 8):
            if 0 <= r < rows:
                PC[r] = PC[r] + E0[e]
    sweep(PC, PA, F, 1, rows - 1, 1, 1)
    sweep(PA, PB, F, 2, rows - 2, 1, 1)

    def out_row(x):
        r = OFF + x
        p = PB[r]
        pre_out[x] = p[0:own_y]
        gx = (0.5 * STEP) * (PB[r + 1] - PB[r - 1])
        gy = (0.5 * STEP) * (roll(p, -1, 0) - roll(p, 1, 0))
        gz = STEP * (jnp.where(last, p, roll(p, -1, 1)) - jnp.where(first, p, roll(p, 1, 1)))
        for a, g in enumerate((gx, gy, gz)):
            vel_out[a, x] = (S[a, r] - g)[0:own_y]

    loop(0, own_x, out_row)


def per_device(nx, ny, velocity, pressure, land_type, turbine_cells, surface_drag):
    _, own_x, own_y, nz = velocity.shape
    kinds = jnp.arange(surface_drag.shape[0], dtype=jnp.int32)
    ground = jnp.sum(jnp.where(land_type.T[:, :, None] == kinds, surface_drag, 0.0), axis=-1)
    ground = jnp.pad(ground, ((0, 0), (0, nz - own_x)))
    side = (own_y // 8 + 1) * 8
    rows = own_x + 2 * OFF
    window = pltpu.VMEM((rows, side, nz), F32)

    def rims(width, *lead):
        rim = pltpu.VMEM((*lead, own_x + 2 * width, width, nz), F32)
        stage = pltpu.VMEM((*lead, own_x, width, nz), F32)
        return [rim, rim, stage, stage]

    three = pltpu.VMEM((3, rows, side, nz), F32)
    half, quarter = own_x // 2, own_x // 4
    y1 = own_y // 2
    full1, full2 = ny * y1, ny * y1 // 2
    packed = half // 2
    level1 = pltpu.VMEM((2 * (packed + 6), full1, nz), F32)
    rows2 = quarter * (2 * REACH + 1)
    level2 = pltpu.VMEM((rows2, full2, nz), F32)
    level3 = pltpu.VMEM((rows2 // 2, full2, nz), F32)
    count = 5 * 8 + 3 * ny - 1 + 2 * REACH
    scratch = [three] + rims(3, 3) + [window] + rims(1) + [window] + rims(3)
    scratch += [window, window] + rims(3) + [window] + rims(2) + [three, three]
    scratch += [
        pltpu.VMEM((half, own_y, nz), F32),
        pltpu.VMEM((quarter, full1, nz), F32),
        pltpu.VMEM((own_x, own_y, nz), jnp.int32),
        pltpu.VMEM((own_y, nz), F32),
        pltpu.VMEM((ny, packed + 6, y1, nz), F32),
        level1, level1, level1,
        pltpu.VMEM((2 * REACH + 1, full2, nz), F32),
        level2, level2, level2, level3, level3, level3,
        pltpu.VMEM((8, full1, nz), F32),
        pltpu.VMEM((12, side, nz), F32),
        pltpu.SemaphoreType.DMA((4,)),
        pltpu.SemaphoreType.DMA((count,)),
        pltpu.SemaphoreType.DMA((count,)),
    ]
    anywhere = pl.BlockSpec(memory_space=pl.ANY)
    inside = pl.BlockSpec(memory_space=pltpu.VMEM)
    return tuple(
        pl.pallas_call(
            functools.partial(kernel, nx, ny),
            out_shape=(
                jax.ShapeDtypeStruct(velocity.shape, F32),
                jax.ShapeDtypeStruct(pressure.shape, F32),
            ),
            in_specs=[anywhere] * 4,
            out_specs=(inside, inside),
            scratch_shapes=scratch,
            compiler_params=pltpu.CompilerParams(collective_id=0, has_side_effects=True),
        )(velocity, pressure, turbine_cells, ground)
    )


def solution(mesh):
    in_specs = (
        P(None, "gx", "gy", None),
        P("gx", "gy", None),
        P("gx", "gy"),
        P("gx", "gy", None),
        P(),
    )
    out_specs = (P(None, "gx", "gy", None), P("gx", "gy", None))
    body = functools.partial(per_device, mesh.shape["gx"], mesh.shape["gy"])
    return jax.shard_map(
        body, mesh=mesh, in_specs=in_specs, out_specs=out_specs, check_vma=False
    )
```

time: 221 us -> 58.2 us (0.26)
  waiting for transfers between devices: 122 us -> 0 us
  starting transfers between devices: 54.4 us -> 0 us
  Pallas kernels: 0 us -> 53.3 us
  other arithmetic: 17.7 us -> 0.19 us
  local copies, waits for them, and re-layouts: 20.3 us -> 3.84 us
  blocking collectives: 4.36 us -> 0 us
    ppermute x68 -> x0, waiting for transfers between devices: 122 us -> none  [the longest x34 91.8 us: with_halo(): lax.ppermute(lax.slice_in_dim(block, block.shape[dim] - width, None, axis...]
    ppermute x68 -> x0, starting transfers between devices: 54.4 us -> none  [the longest x34 34.9 us: with_halo(): lax.ppermute(lax.slice_in_dim(block, 0, width, axis=dim), axis, backward)]
    pallas_call x0 -> x1, Pallas kernels: none -> 53.3 us  [per_device(): pl.pallas_call(functools.partial(kernel, nx, ny), out_shape=(jax.ShapeDty...]
    reshape x8 -> x0, local copies, waits for them, and re-layouts: 12 us -> none  [the longest x3 11 us: coarsen(): values.reshape(values.shape[0] // 2, 2, values.shape[1] // 2, 2, values.s...]
    reduce_sum x5 -> x1, other arithmetic: 5.29 us -> 0.19 us  [per_device(): jnp.sum(jnp.where(land_type.T[:, :, None] == kinds, surface_drag, 0.0), a...]
    all_gather x1 -> x0, blocking collectives: 4.36 us -> none  [per_device(): source_two = lax.all_gather(local_two, 'gy', axis=1, tiled=True)]
    slice x56 -> x0, local copies, waits for them, and re-layouts: 4.33 us -> none  [the longest x15 1.63 us: strip(): padded = jnp.pad(padded, ((0, 0), (1, 1), (0, 0)), mode='wrap')]
    mul x4 -> x0, other arithmetic: 2.99 us -> none  [the longest x1 1.96 us: central(): (shifted(values, axis_pos, 1) - shifted(values, axis_pos, -1)) * (0.5 / s...]
  transfers between devices with their start and end apart: 68 -> 0, of which waited for: 57 -> 0; matrix products, arithmetic and copies ran while one was open for 6% -> 0% of each run, Pallas kernels for 0% -> 0%
where the time goes in v1:
time: 58.2 us; the launch traced here: 57.9 us
  Pallas kernels  53.3 us (92%)
  local copies, waits for them, and re-layouts  3.84 us (7%)
  between operations  0.66 us (1%)
    pallas_call x1, Pallas kernels, per_device(): pl.pallas_call(functools.partial(kernel, nx, ny), out_shape=(jax.ShapeDty...  53.3 us
    unnamed x6, local copies, waits for them, and re-layouts  2.47 us

profile of v1, /device:TPU:0, one launch (start us, length us, event | category | flops | bytes accessed | tf_op | source)
XLA Modules:
  0.0 57.9 jit_solution(3346582749439711324)
XLA Ops:
  0.6 0.0 copy-start.1
  0.6 0.8 %copy.8 = s32[16,16]{1,0:T(8,128)S(1)} copy(s32[16,16]{0,1:T(8,128)} %bitcast.1) | data formatting | bytes 2048 | tf_op jit(solution)/shard_map/transpose | solution.py:358
  1.4 0.0 copy-done.1
  1.4 0.2 select_reduce_fusion
  1.6 0.6 %pad.4.ground_in = f32[16,128]{1,0:T(8,128)} pad(f32[16,16]{1,0:T(8,128)S(1)} %select_reduce_fusion, f32[]{:T(128)} %constant.1.clone.1), padding=0_0x0_112 | pad | bytes 9220 | tf_op jit(solution)/shard_map/jit(_pad)/pad | solution.py:359
  2.2 53.3 %shard_map.68 = (f32[3,16,16,128]{3,2,1,0:T(8,128)}, f32[16,16,128]{2,1,0:T(8,128)}) custom-call(f32[3,16,16,128]{3,2,1,0:T(8,128)} %vel_in.1, f32[16,16,128]{2,1,0:T(8,128)} %pre_in.1, s32[16,16,128]{2,1,0:T(8,128)} %turb_in.1, f32[16,128]{1,0:T(8,128)} %pad.4.ground_in), custom_call_target="tpu_custom_call" | custom-call | tf_op jit(solution)/shard_map/pallas_call | solution.py:399
  55.5 0.0 copy-start
  55.5 1.8 %copy.11 = f32[3,16,16,128]{3,2,1,0:T(8,128)} copy(f32[3,16,16,128]{3,2,1,0:T(8,128)} %get-tuple-element.4) | data formatting | bytes 786432
  57.3 0.0 copy-done
  57.3 0.7 %copy.12 = f32[16,16,128]{2,1,0:T(8,128)} copy(f32[16,16,128]{2,1,0:T(8,128)S(1)} %copy-done) | data formatting | bytes 262144
Async XLA Ops:
  0.6 0.8 %copy-start.1 = (f32[16]{0:T(128)S(1)}, f32[16]{0:T(128)}, u32[]{:S(2)}) copy-start(f32[16]{0:T(128)} %param.9) | copy-start | bytes 196
  55.5 1.8 %copy-start = (f32[16,16,128]{2,1,0:T(8,128)S(1)}, f32[16,16,128]{2,1,0:T(8,128)}, u32[]{:S(2)}) copy-start(f32[16,16,128]{2,1,0:T(8,128)} %get-tuple-element.5) | copy-start | bytes 393220

commit v2 on v1

--- a/solution.py
+++ b/solution.py
@@ -13,21 +13,36 @@
 WEIGHT = 0.8 / 12.0
 KEEP = 0.2
 OFF = 3
+G_STRESS = 4
+G_FINE = 8
+VMEM_LIMIT = 60 * 1024 * 1024
 REACH = 4
 
 
-def loop(low, high, body):
-    def step(index, carry):
-        body(index)
-        return carry
-
-    lax.fori_loop(low, high, step, 0)
+def loop(low, high, body, group):
+    def run(indices):
+        found = [store for index in indices for store in body(index)]
+        for ref, at, value in found:
+            ref[at] = value
+
+    whole = (high - low) // group
+    if whole == 1:
+        run(range(low, low + group))
+    elif whole > 1:
+
+        def step(index, carry):
+            run([low + index * group + k for k in range(group)])
+            return carry
+
+        lax.fori_loop(0, whole, step, 0)
+    if low + whole * group < high:
+        run(range(low + whole * group, high))
 
 
 def kernel(
-    nx, ny, vel_in, pre_in, turb_in, ground_in, vel_out, pre_out,
+    nx, ny, vel_in, pre_in, turb_in, land_in, coeff_in, vel_out, pre_out,
     W, WLO, WHI, WSL, WSH, D, DLO, DHI, DSL, DSH, PA, PLO, PHI, PSL, PSH,
-    PB, PC, CLO, CHI, CSL, CSH, F, FLO, FHI, FSL, FSH, T, S, tmp, tmp2, turb, ground,
+    PB, PC, CLO, CHI, CSL, CSH, F, FLO, FHI, FSL, FSH, T, S, tmp, tmp2, turb, land, coeff,
     G1, F1, P1A, P1B, G2, F2, P2A, P2B, F3, P3A, P3B, E1, E0,
     load_sem, send_sem, recv_sem,
 ):
@@ -40,7 +55,8 @@
         pltpu.make_async_copy(vel_in, W.at[:, OFF : OFF + own_x, 0:own_y], load_sem.at[0]),
         pltpu.make_async_copy(pre_in, PA.at[OFF : OFF + own_x, 0:own_y], load_sem.at[1]),
         pltpu.make_async_copy(turb_in, turb, load_sem.at[2]),
-        pltpu.make_async_copy(ground_in, ground, load_sem.at[3]),
+        pltpu.make_async_copy(land_in, land, load_sem.at[3]),
+        pltpu.make_async_copy(coeff_in, coeff, load_sem.at[4]),
     ]
     for load in loads:
         load.start()
@@ -50,8 +66,9 @@
 
     friends = [(dx, 0) for dx in range(-REACH, REACH + 1) if dx != 0]
     friends += [(dx, dy) for dx in (-1, 0, 1) for dy in range(1, ny)]
+    close = [(dx, dy) for dx, dy in friends if abs(dx) < 2]
     barrier = pltpu.get_barrier_semaphore()
-    for dx, dy in friends:
+    for dx, dy in close:
         pl.semaphore_signal(barrier, inc=1, device_id=device(dx, dy), device_id_type=MESH)
 
     used = [0]
@@ -124,15 +141,23 @@
     def roll(v, shift, axis):
         return pltpu.roll(v, shift % v.shape[axis], axis)
 
+    shape = (own_y, own_y)
+    diagonal = lax.broadcasted_iota(jnp.int32, shape, 0) == lax.broadcasted_iota(jnp.int32, shape, 1)
     lane16 = lane_of(own_y)
+    loads[3].wait()
+    loads[4].wait()
+    kinds = land[...]
+    ground = jnp.zeros(kinds.shape, F32)
+    for kind in range(coeff.shape[0]):
+        ground = jnp.where(kinds == kind, coeff[kind], ground)
     loads[2].wait()
-    loads[3].wait()
     for x in range(own_x):
-        low = jnp.where(lane16 == 0, roll(ground[...], -x, 1), 0.0)
+        column = jnp.sum(jnp.where(diagonal, ground[x : x + 1, :], 0.0), axis=1, keepdims=True)
+        low = jnp.where(lane16 == 0, column, 0.0)
         D[OFF + x, 0:own_y, :] = 2.0 * turb[x].astype(F32) + low
     loads[0].wait()
     loads[1].wait()
-    pl.semaphore_wait(barrier, len(friends))
+    pl.semaphore_wait(barrier, len(close))
     w_copies = send_y(W, WLO, WHI, WSL, WSH, 3, True) + send_x(W, 3, True)
     d_copies = send_y(D, DLO, DHI, DSL, DSH, 1) + send_x(D, 1)
     p_copies = send_y(PA, PLO, PHI, PSL, PSH, 3) + send_x(PA, 3)
@@ -164,9 +189,7 @@
         flat = v[0] * v[0] + v[1] * v[1]
         ghost = 0.03 * jnp.sqrt(2.0 * v[2] * v[2] + flat)
         ghosts = [ghost * v[0], ghost * v[1], (ghost + ghost) * v[2]]
-        T[0, r] = t00
-        T[1, r] = t01
-        T[2, r] = t02
+        out = [(T, (0, r), t00), (T, (1, r), t01), (T, (2, r), t02)]
         drag = D[r] * jnp.sqrt(flat)
         for a, (ty, tz) in enumerate(((t01, t02), (t11, t12), (t12, t22))):
             change = 0.5 * (roll(ty, -1, 0) - roll(ty, 1, 0))
@@ -176,22 +199,24 @@
                 change -= drag * v[a]
             if a == 0:
                 change += 1.0
-            S[a, r] = v[a] + STEP * change
-
-    loop(1, rows - 1, stress_row)
+            out.append((S, (a, r), v[a] + STEP * change))
+        return out
+
+    loop(1, rows - 1, stress_row, G_STRESS)
 
     def star_row(r):
-        for a in range(3):
-            S[a, r] = S[a, r] + (0.5 * STEP) * (T[a, r + 1] - T[a, r - 1])
-
-    loop(2, rows - 2, star_row)
+        return [
+            (S, (a, r), S[a, r] + (0.5 * STEP) * (T[a, r + 1] - T[a, r - 1])) for a in range(3)
+        ]
+
+    loop(2, rows - 2, star_row, G_FINE)
 
     def source_row(r):
         s1, s2 = S[1, r], S[2, r]
         flat = 0.5 * (S[0, r + 1] - S[0, r - 1] + roll(s1, -1, 0) - roll(s1, 1, 0))
-        F[r] = (flat + up0(s2) - down0(s2)) / STEP
-
-    loop(OFF, OFF + own_x, source_row)
+        return [(F, r, (flat + up0(s2) - down0(s2)) / STEP)]
+
+    loop(OFF, OFF + own_x, source_row, G_FINE)
     f_copies = send_y(F, FLO, FHI, FSL, FSH, 2) + send_x(F, 2)
     finish(p_copies)
     place(PA, PLO, PHI, 3)
@@ -205,12 +230,12 @@
         s = src[r + 1] + src[r - 1] + roll(p, -sy, 0) + roll(p, sy, 0)
         return p, s + 4.0 * z
 
-    def sweep(src, dst, f, low, high, sy, sz):
+    def sweep(src, dst, f, low, high, sy, sz, group=64):
         def body(r):
             p, around = stencil(src, r, sy, sz)
-            dst[r] = KEEP * p + WEIGHT * (around - f[r])
-
-        loop(low, high, body)
+            return [(dst, r, KEEP * p + WEIGHT * (around - f[r]))]
+
+        loop(low, high, body, min(group, high - low))
 
     def residual(src, f, r, sy, sz):
         p, around = stencil(src, r, sy, sz)
@@ -225,8 +250,8 @@
         at = (lane_of(v.shape[0]) // stride) % 2
         return jnp.where(at == bit, v, roll(v, stride if bit == 0 else -stride, 1))
 
-    sweep(PA, PB, F, 1, rows - 1, 1, 1)
-    sweep(PB, PA, F, 2, rows - 2, 1, 1)
+    sweep(PA, PB, F, 1, rows - 1, 1, 1, G_FINE)
+    sweep(PB, PA, F, 2, rows - 2, 1, 1, G_FINE)
     PC[OFF : OFF + own_x, 0:own_y, :] = PA[OFF : OFF + own_x, 0:own_y, :]
 
     half = own_x // 2
@@ -235,9 +260,9 @@
     def fine_residual(i):
         r = OFF + 2 * i
         v = residual(PA, F, r, 1, 1) + residual(PA, F, r + 1, 1, 1)
-        tmp[i] = pair(v[0:own_y], 1, 1)
-
-    loop(0, half, fine_residual)
+        return [(tmp, i, pair(v[0:own_y], 1, 1))]
+
+    loop(0, half, fine_residual, 2)
     packed = half // 2
     lane8 = lane_of(y1)
     for i in range(packed):
@@ -293,10 +318,9 @@
     def coarse_source(i):
         v = residual(P2B, F2, 2 * i, 1, 4) + residual(P2B, F2, 2 * i + 1, 1, 4)
         f = 0.5 * pair(pair(v, 4, 1), 1, 0)
-        F3[i] = f
-        P3A[i] = -WEIGHT * f
-
-    loop(1, rows2 // 2 - 1, coarse_source)
+        return [(F3, i, f), (P3A, i, -WEIGHT * f)]
+
+    loop(1, rows2 // 2 - 1, coarse_source, rows2 // 2 - 2)
     sweep(P3A, P3B, F3, 2, 16, 2, 8)
     sweep(P3B, P3A, F3, 3, 15, 2, 8)
     sweep(P3A, P3B, F3, 4, 14, 2, 8)
@@ -304,10 +328,9 @@
     def line_row(r):
         mean = jnp.mean(residual(P3B, F3, r, 2, 8), axis=0, keepdims=True)
         v = P3B[r] - WEIGHT * mean
-        P2B[2 * r] = P2B[2 * r] + v
-        P2B[2 * r + 1] = P2B[2 * r + 1] + v
-
-    loop(6, 12, line_row)
+        return [(P2B, x, P2B[x] + v) for x in (2 * r, 2 * r + 1)]
+
+    loop(6, 12, line_row, 6)
     sweep(P2B, P2A, F2, 13, 23, 1, 4)
 
     def second_row(m):
@@ -336,27 +359,25 @@
         for r in (2 * m - 9, 2 * m - 8):
             if 0 <= r < rows:
                 PC[r] = PC[r] + E0[e]
-    sweep(PC, PA, F, 1, rows - 1, 1, 1)
-    sweep(PA, PB, F, 2, rows - 2, 1, 1)
+    sweep(PC, PA, F, 1, rows - 1, 1, 1, G_FINE)
+    sweep(PA, PB, F, 2, rows - 2, 1, 1, G_FINE)
 
     def out_row(x):
         r = OFF + x
         p = PB[r]
-        pre_out[x] = p[0:own_y]
+        out = [(pre_out, x, p[0:own_y])]
         gx = (0.5 * STEP) * (PB[r + 1] - PB[r - 1])
         gy = (0.5 * STEP) * (roll(p, -1, 0) - roll(p, 1, 0))
         gz = STEP * (jnp.where(last, p, roll(p, -1, 1)) - jnp.where(first, p, roll(p, 1, 1)))
         for a, g in enumerate((gx, gy, gz)):
-            vel_out[a, x] = (S[a, r] - g)[0:own_y]
-
-    loop(0, own_x, out_row)
+            out.append((vel_out, (a, x), (S[a, r] - g)[0:own_y]))
+        return out
+
+    loop(0, own_x, out_row, 2)
 
 
 def per_device(nx, ny, velocity, pressure, land_type, turbine_cells, surface_drag):
     _, own_x, own_y, nz = velocity.shape
-    kinds = jnp.arange(surface_drag.shape[0], dtype=jnp.int32)
-    ground = jnp.sum(jnp.where(land_type.T[:, :, None] == kinds, surface_drag, 0.0), axis=-1)
-    ground = jnp.pad(ground, ((0, 0), (0, nz - own_x)))
     side = (own_y // 8 + 1) * 8
     rows = own_x + 2 * OFF
     window = pltpu.VMEM((rows, side, nz), F32)
@@ -382,18 +403,18 @@
         pltpu.VMEM((half, own_y, nz), F32),
         pltpu.VMEM((quarter, full1, nz), F32),
         pltpu.VMEM((own_x, own_y, nz), jnp.int32),
-        pltpu.VMEM((own_y, nz), F32),
+        pltpu.VMEM(land_type.shape, jnp.int32),
+        pltpu.SMEM(surface_drag.shape, F32),
         pltpu.VMEM((ny, packed + 6, y1, nz), F32),
         level1, level1, level1,
         pltpu.VMEM((2 * REACH + 1, full2, nz), F32),
         level2, level2, level2, level3, level3, level3,
         pltpu.VMEM((8, full1, nz), F32),
         pltpu.VMEM((12, side, nz), F32),
-        pltpu.SemaphoreType.DMA((4,)),
+        pltpu.SemaphoreType.DMA((5,)),
         pltpu.SemaphoreType.DMA((count,)),
         pltpu.SemaphoreType.DMA((count,)),
     ]
-    anywhere = pl.BlockSpec(memory_space=pl.ANY)
     inside = pl.BlockSpec(memory_space=pltpu.VMEM)
     return tuple(
         pl.pallas_call(
@@ -402,11 +423,13 @@
                 jax.ShapeDtypeStruct(velocity.shape, F32),
                 jax.ShapeDtypeStruct(pressure.shape, F32),
             ),
-            in_specs=[anywhere] * 4,
+            in_specs=[pl.BlockSpec(memory_space=pltpu.HBM)] * 5,
             out_specs=(inside, inside),
             scratch_shapes=scratch,
-            compiler_params=pltpu.CompilerParams(collective_id=0, has_side_effects=True),
-        )(velocity, pressure, turbine_cells, ground)
+            compiler_params=pltpu.CompilerParams(
+                collective_id=0, has_side_effects=True, vmem_limit_bytes=VMEM_LIMIT
+            ),
+        )(velocity, pressure, turbine_cells, land_type, surface_drag)
     )
 
 

time: 58.2 us -> 35.5 us (0.61)
  Pallas kernels: 53.3 us -> 32.3 us
  local copies, waits for them, and re-layouts: 3.84 us -> 2.46 us
    pallas_call x1, Pallas kernels: 53.3 us -> 32.3 us  [per_device(): pl.pallas_call(functools.partial(kernel, nx, ny), out_shape=(jax.ShapeDty...]
    transpose x1 -> x0, local copies, waits for them, and re-layouts: 0.77 us -> none  [per_device(): land_type.T[:, :, None] == kinds]
    pad x1 -> x0, local copies, waits for them, and re-layouts: 0.61 us -> none  [per_device(): ground = jnp.pad(ground, ((0, 0), (0, nz - own_x)))]
    unnamed x6 -> x4, local copies, waits for them, and re-layouts: 2.47 us -> 2.46 us
where the time goes in v2:
time: 35.5 us; the launch traced here: 35.4 us
  Pallas kernels  32.3 us (91%)
  local copies, waits for them, and re-layouts  2.46 us (7%)
  between operations  0.65 us (2%)
    pallas_call x1, Pallas kernels, per_device(): pl.pallas_call(functools.partial(kernel, nx, ny), out_shape=(jax.ShapeDty...  32.3 us
    unnamed x4, local copies, waits for them, and re-layouts  2.46 us

profile of v2, /device:TPU:0, one launch (start us, length us, event | category | flops | bytes accessed | tf_op | source)
XLA Modules:
  0.0 35.4 jit_solution(299386975650397485)
XLA Ops:
  0.6 32.3 %shard_map.68 = (f32[3,16,16,128]{3,2,1,0:T(8,128)}, f32[16,16,128]{2,1,0:T(8,128)}) custom-call(f32[3,16,16,128]{3,2,1,0:T(8,128)} %vel_in.1, f32[16,16,128]{2,1,0:T(8,128)} %pre_in.1, s32[16,16,128]{2,1,0:T(8,128)} %turb_in.1, s32[16,16]{1,0:T(8,128)} %land_in.1, f32[16]{0:T(128)} %coeff_in.1), custom_call_target="tpu_custom_call" | custom-call | tf_op jit(solution)/shard_map/pallas_call | solution.py:420
  32.9 0.0 copy-start
  32.9 1.8 %copy.9 = f32[3,16,16,128]{3,2,1,0:T(8,128)} copy(f32[3,16,16,128]{3,2,1,0:T(8,128)} %get-tuple-element.4) | data formatting | bytes 786432
  34.7 0.0 copy-done
  34.7 0.7 %copy.10 = f32[16,16,128]{2,1,0:T(8,128)} copy(f32[16,16,128]{2,1,0:T(8,128)S(1)} %copy-done) | data formatting | bytes 262144
Async XLA Ops:
  32.9 1.8 %copy-start = (f32[16,16,128]{2,1,0:T(8,128)S(1)}, f32[16,16,128]{2,1,0:T(8,128)}, u32[]{:S(2)}) copy-start(f32[16,16,128]{2,1,0:T(8,128)} %get-tuple-element.5) | copy-start | bytes 393220

commit v3 on v2

--- a/solution.py
+++ b/solution.py
@@ -416,7 +416,7 @@
         pltpu.SemaphoreType.DMA((count,)),
     ]
     inside = pl.BlockSpec(memory_space=pltpu.VMEM)
-    return tuple(
+    moved = tuple(
         pl.pallas_call(
             functools.partial(kernel, nx, ny),
             out_shape=(
@@ -431,6 +431,24 @@
             ),
         )(velocity, pressure, turbine_cells, land_type, surface_drag)
     )
+    parts = 2
+    vel_block = pl.BlockSpec((3, own_x // parts, own_y, nz), lambda i: (0, i, 0, 0))
+    pre_block = pl.BlockSpec((own_x // parts, own_y, nz), lambda i: (i, 0, 0))
+    return pl.pallas_call(
+        hand_over,
+        grid=(parts,),
+        out_shape=(
+            jax.ShapeDtypeStruct(velocity.shape, F32),
+            jax.ShapeDtypeStruct(pressure.shape, F32),
+        ),
+        in_specs=[vel_block, pre_block],
+        out_specs=(vel_block, pre_block),
+    )(*moved)
+
+
+def hand_over(vel_in, pre_in, vel_out, pre_out):
+    vel_out[...] = vel_in[...]
+    pre_out[...] = pre_in[...]
 
 
 def solution(mesh):

time: 35.5 us -> 34.8 us (0.980)
  local copies, waits for them, and re-layouts: 2.46 us -> 0 us
  Pallas kernels: 32.3 us -> 34 us
    unnamed x4 -> x0, local copies, waits for them, and re-layouts: 2.46 us -> none
    pallas_call x0 -> x1, Pallas kernels: none -> 1.79 us  [per_device(): pl.pallas_call(hand_over, grid=(parts,), out_shape=(jax.ShapeDtypeStruct(...]
where the time goes in v3:
time: 34.8 us; the launch traced here: 34.7 us
  Pallas kernels  34 us (98%)
  between operations  0.64 us (2%)
    pallas_call x1, Pallas kernels, per_device(): pl.pallas_call(functools.partial(kernel, nx, ny), out_shape=(jax.ShapeDty...  32.3 us
    pallas_call x1, Pallas kernels, per_device(): pl.pallas_call(hand_over, grid=(parts,), out_shape=(jax.ShapeDtypeStruct(...  1.79 us

profile of v3, /device:TPU:0, one launch (start us, length us, event | category | flops | bytes accessed | tf_op | source)
XLA Modules:
  0.0 34.7 jit_solution(2361037085961184704)
XLA Ops:
  0.6 32.3 %shard_map.68 = (f32[3,16,16,128]{3,2,1,0:T(8,128)}, f32[16,16,128]{2,1,0:T(8,128)}) custom-call(f32[3,16,16,128]{3,2,1,0:T(8,128)} %vel_in.1, f32[16,16,128]{2,1,0:T(8,128)} %pre_in.1, s32[16,16,128]{2,1,0:T(8,128)} %turb_in.1, s32[16,16]{1,0:T(8,128)} %land_in.1, f32[16]{0:T(128)} %coeff_in.1), custom_call_target="tpu_custom_call" | custom-call | tf_op jit(solution)/shard_map/pallas_call | solution.py:420
  32.9 1.8 %shard_map.69 = (f32[3,16,16,128]{3,2,1,0:T(8,128)}, f32[16,16,128]{2,1,0:T(8,128)}) custom-call(f32[3,16,16,128]{3,2,1,0:T(8,128)} %get-tuple-element.4.vel_in, f32[16,16,128]{2,1,0:T(8,128)} %get-tuple-element.5.pre_in), custom_call_target="tpu_custom_call" | custom-call | tf_op jit(solution)/shard_map/pallas_call | solution.py:437
